TPU v7x, 32 devices: a whole 2x2x4 slice. The times are simulated.
32 devices in a mesh: long: 8 (over y, x, core), short: 4 (over z).
Axes of the slice: x: 2, y: 2, z: 4, core: 2. Of those that a mesh axis runs over, the one named last changes fastest.
Arguments:
- transition: float32 [64, 384, 384], P(('long', 'short')), may hold values from 0 to 1
- innovation: float32 [64, 384], P(('long', 'short')), may hold values from 20 to 80
- observation: float32 [64, 384], P(('long', 'short')), may hold values from 0.05 to 0.5
- effects: float32 [64, 384, 384], P(('long', 'short')), may hold values from -0.0045 to 0.0045
- prior: float32 [384], replicated, may hold values from 0.5 to 2
- right_side: float32 [64, 384, 128], P(('long', 'short')), may hold values from -3 to 3
- tip_right: float32 [384, 128], replicated, may hold values from -6 to 6
Outputs:
- solution: float32 [64, 384, 128], P(('long', 'short'))
- tip_solution: float32 [384, 128], replicated
All inputs are finite; a program needn't handle non-finite values.
Results may differ from a plain program's by a relative error of at most 0.0003.
Values sent between devices are 32-bit elements; how exact they have to be, the bound alone decides.
A program may use at most 256 MiB of HBM per device.

v0:
```python
import jax
import jax.numpy as jnp
from jax import lax
from jax.sharding import PartitionSpec as P

HIGHEST = lax.Precision.HIGHEST


def shifted(block, axis, distance):
    devices = range(lax.axis_size(axis))
    route = [(i - distance, i) for i in devices if i - distance in devices]
    return lax.ppermute(block, axis, route)


def gram_prod(left, right):
    return jnp.einsum("ji,jk->ik", left, right, precision=HIGHEST)


def mat_prod(left, right):
    return jnp.matmul(left, right, precision=HIGHEST)


def solve_lower(factor, values):
    return jax.scipy.linalg.solve_triangular(factor, values, lower=True)


def solve_upper(factor, values):
    return jax.scipy.linalg.solve_triangular(factor, values, lower=True, trans=1)


def move_near(values, offset):
    return shifted(values, ("long", "short"), offset)


def move_far(values, offset):
    return shifted(values, "long", offset)


def reduce_level(state, distance, index, total, active, mover, tip_width):
    node_diag, node_couple, node_arrow, node_rhs, tip_terms, tip_rhs_terms = state
    node_width = node_diag.shape[0]
    side_count = node_rhs.shape[1]
    rank_one = index + 1
    alive = jnp.logical_and(active, rank_one % distance == 0)
    drop = jnp.logical_and(alive, rank_one // distance % 2 == 1)
    keep = jnp.logical_and(alive, jnp.logical_not(drop))
    from_left = jnp.logical_and(keep, index - distance >= 0)
    from_right = jnp.logical_and(keep, index + distance <= total - 1)
    identity = jnp.eye(node_width, dtype=jnp.float32)
    full_width = 2 * node_width + tip_width + side_count
    part_width = node_width + tip_width + side_count
    tip_zero = jnp.zeros((tip_width, tip_width + side_count), jnp.float32)
    right_couple = mover(node_couple, -distance)

    def eliminate(operands):
        diag_item, couple_item, right_item, arrow_item, rhs_item = operands
        factor = jnp.linalg.cholesky(diag_item)
        solved = solve_lower(
            factor, jnp.concatenate([couple_item, right_item.T, arrow_item, rhs_item], axis=1)
        )
        part_left = solved[:, :node_width]
        rest = solved[:, 2 * node_width :]
        toward_left = gram_prod(part_left, jnp.concatenate([part_left, rest], axis=1))
        toward_right = gram_prod(solved[:, node_width : 2 * node_width], solved)
        tip_part = gram_prod(rest[:, :tip_width], rest)
        return (factor, solved, toward_left, toward_right, tip_part)

    def skip(operands):
        return (
            identity,
            jnp.zeros((node_width, full_width), jnp.float32),
            jnp.zeros((node_width, part_width), jnp.float32),
            jnp.zeros((node_width, full_width), jnp.float32),
            tip_zero,
        )

    factor, solved, toward_left, toward_right, tip_part = lax.cond(
        drop, eliminate, skip, (node_diag, node_couple, right_couple, node_arrow, node_rhs)
    )
    left_update = mover(toward_right, distance)
    saved = (
        factor,
        solved[:, :node_width],
        solved[:, node_width : 2 * node_width],
        solved[:, 2 * node_width : 2 * node_width + tip_width],
        solved[:, 2 * node_width + tip_width :],
        None,
        drop,
    )
    right_update = mover(toward_left, -distance)
    right_gate = jnp.where(from_right, 1.0, 0.0)
    left_gate = jnp.where(from_left, 1.0, 0.0)
    arrow_end = 2 * node_width + tip_width
    node_diag = (
        node_diag
        - right_gate * right_update[:, :node_width]
        - left_gate * left_update[:, node_width : 2 * node_width]
    )
    node_couple = jnp.where(from_left, -left_update[:, :node_width], node_couple)
    node_arrow = (
        node_arrow
        - right_gate * right_update[:, node_width : node_width + tip_width]
        - left_gate * left_update[:, 2 * node_width : arrow_end]
    )
    node_rhs = (
        node_rhs
        - right_gate * right_update[:, node_width + tip_width :]
        - left_gate * left_update[:, arrow_end:]
    )
    tip_terms = tip_terms - tip_part[:, :tip_width]
    tip_rhs_terms = tip_rhs_terms - tip_part[:, tip_width:]
    return ((node_diag, node_couple, node_arrow, node_rhs, tip_terms, tip_rhs_terms), saved)


def unwind_level(node_x, saved, tip_solution, mover, distance):
    factor, part_left, part_right, part_arrow, part_rhs, link, drop = saved
    left_x = mover(node_x, distance)
    right_term = mat_prod(part_right, mover(node_x, -distance))
    value = part_rhs - mat_prod(part_left, left_x) - right_term - mat_prod(part_arrow, tip_solution)
    return jnp.where(drop, solve_upper(factor, value), node_x)


def body(transition, innovation, observation, effects, prior, right_side, tip_right):
    block_count, node_width = innovation.shape
    tip_width = prior.shape[0]
    side_count = right_side.shape[2]
    device_count = lax.axis_size(("long", "short"))
    short_count = lax.axis_size("short")
    long_count = lax.axis_size("long")
    position = lax.axis_index(("long", "short"))
    long_place = lax.axis_index("long")
    short_place = lax.axis_index("short")
    identity = jnp.eye(node_width, dtype=jnp.float32)
    weighted_trans = innovation[:, :, None] * transition
    weighted_effect = innovation[:, :, None] * effects
    succ_diag = jnp.einsum("tji,tjk->tik", transition, weighted_trans, precision=HIGHEST)
    succ_arrow = jnp.einsum("tji,tjk->tik", transition, weighted_effect, precision=HIGHEST)
    tip_terms = jnp.einsum("tji,tjk->ik", effects, weighted_effect, precision=HIGHEST)
    global_block = position * block_count + jnp.arange(block_count)
    couple = -weighted_trans * jnp.where(global_block == 0, 0.0, 1.0)[:, None, None]
    diag_base = (innovation + observation)[:, :, None] * identity
    interior = block_count - 1
    own_diag = diag_base[:interior] + succ_diag[1:]
    own_arrow = -weighted_effect[:interior] + succ_arrow[1:]
    order = jnp.arange(interior)
    first = (order == 0)[:, None, None]
    last = (order == interior - 1)[:, None, None]
    left_cols = jnp.where(first, couple[0][None], 0.0)
    sep_cols = jnp.where(last, couple[interior].T[None], 0.0)
    previous = jnp.where(first, 0.0, couple[:interior])
    columns = jnp.concatenate([left_cols, sep_cols, own_arrow, right_side[:interior]], axis=2)
    span = 2 * node_width + tip_width
    full_width = span + side_count

    def forward(carry, items):
        factor_prev, solved_prev, gram = carry
        diag_item, prev_item, column_item = items
        link = solve_lower(factor_prev, prev_item.T)
        factor = jnp.linalg.cholesky(diag_item - gram_prod(link, link))
        solved = solve_lower(factor, column_item - gram_prod(link, solved_prev))
        gram = gram + gram_prod(solved[:, :span], solved)
        return ((factor, solved, gram), (factor, link, solved))

    start = (
        identity,
        jnp.zeros((node_width, full_width), jnp.float32),
        jnp.zeros((span, full_width), jnp.float32),
    )
    final_carry, stored = lax.scan(forward, start, (own_diag, previous, columns))
    gram = final_carry[2]
    factors, links, solved_all = stored
    left_rows = gram[:node_width]
    sep_rows = gram[node_width : 2 * node_width]
    tip_rows = gram[2 * node_width :]
    left_terms = (
        -left_rows[:, :node_width],
        -left_rows[:, 2 * node_width : span],
        -left_rows[:, span:],
    )
    tip_terms = tip_terms - tip_rows[:, 2 * node_width : span]
    tip_rhs_terms = -tip_rows[:, span:]
    recv_diag, recv_arrow, recv_rhs = move_near(
        (left_terms[0] + succ_diag[0], left_terms[1] + succ_arrow[0], left_terms[2]), -1
    )
    node_diag = diag_base[interior] - sep_rows[:, node_width : 2 * node_width] + recv_diag
    node_couple = -sep_rows[:, :node_width]
    node_arrow = -weighted_effect[interior] - sep_rows[:, 2 * node_width : span] + recv_arrow
    node_rhs = right_side[interior] - sep_rows[:, span:] + recv_rhs
    state = (node_diag, node_couple, node_arrow, node_rhs, tip_terms, tip_rhs_terms)
    always = position >= 0
    lower_saved = []
    for depth in range(short_count.bit_length() - 1):
        state, saved = reduce_level(
            state, 2**depth, position, device_count, always, move_near, tip_width
        )
        lower_saved.append(saved)
    top_row = short_place == short_count - 1
    upper_saved = []
    for depth in range(long_count.bit_length() - 1):
        state, saved = reduce_level(
            state, 2**depth, long_place, long_count, top_row, move_far, tip_width
        )
        upper_saved.append(saved)
    node_diag, node_couple, node_arrow, node_rhs, tip_terms, tip_rhs_terms = state
    final = position == device_count - 1

    def finish(operands):
        diag_item, arrow_item, rhs_item = operands
        factor = jnp.linalg.cholesky(diag_item)
        solved = solve_lower(factor, jnp.concatenate([arrow_item, rhs_item], axis=1))
        return (factor, solved, gram_prod(solved[:, :tip_width], solved))

    def pass_over(operands):
        return (
            identity,
            jnp.zeros((node_width, tip_width + side_count), jnp.float32),
            jnp.zeros((tip_width, tip_width + side_count), jnp.float32),
        )

    final_factor, final_solved, final_tip = lax.cond(
        final, finish, pass_over, (node_diag, node_arrow, node_rhs)
    )
    tip_terms = tip_terms - final_tip[:, :tip_width]
    tip_rhs_terms = tip_rhs_terms - final_tip[:, tip_width:]
    tip_total, tip_rhs_total = lax.psum((tip_terms, tip_rhs_terms), ("long", "short"))
    tip_factor = jnp.linalg.cholesky(tip_total + jnp.diag(prior))
    tip_solution = solve_upper(tip_factor, solve_lower(tip_factor, tip_rhs_total + tip_right))
    final_x = solve_upper(
        final_factor,
        final_solved[:, tip_width:] - mat_prod(final_solved[:, :tip_width], tip_solution),
    )
    node_x = jnp.where(final, final_x, jnp.zeros_like(final_x))
    for depth in reversed(range(len(upper_saved))):
        node_x = unwind_level(node_x, upper_saved[depth], tip_solution, move_far, 2**depth)
    for depth in reversed(range(len(lower_saved))):
        node_x = unwind_level(node_x, lower_saved[depth], tip_solution, move_near, 2**depth)
    left_x = move_near(node_x, 1)
    next_links = jnp.concatenate(
        [links[1:], jnp.zeros((1, node_width, node_width), jnp.float32)], axis=0
    )

    def backward(later, items):
        factor, link_next, solved = items
        value = (
            solved[:, span:]
            - mat_prod(solved[:, :node_width], left_x)
            - mat_prod(solved[:, node_width : 2 * node_width], node_x)
            - mat_prod(solved[:, 2 * node_width : span], tip_solution)
            - mat_prod(link_next, later)
        )
        current = solve_upper(factor, value)
        return (current, current)

    last_value, interior_x = lax.scan(
        backward,
        jnp.zeros((node_width, side_count), jnp.float32),
        (factors, next_links, solved_all),
        reverse=True,
    )
    solution = jnp.concatenate([interior_x, node_x[None]], axis=0)
    return (solution, tip_solution)


def solution(mesh):
    placed = (
        P(("long", "short"), None, None),
        P(("long", "short"), None),
        P(("long", "short"), None),
        P(("long", "short"), None, None),
        P(),
        P(("long", "short"), None, None),
        P(),
    )
    return jax.shard_map(
        body,
        mesh=mesh,
        in_specs=placed,
        out_specs=(P(("long", "short"), None, None), P()),
        check_vma=False,
    )
```

profile of v0, /device:TPU:2, one launch (start us, length us, event | category | flops | bytes accessed | tf_op | source)
XLA Modules:
  0.0 2049.7 jit_solution(13823532065056186043)
XLA Ops:
  13.8 29.7 %custom-call.36 = f32[3,128,128]{1,2,0:T(8,128)S(1)} custom-call(f32[3,128,128]{2,1,0:T(8,128)S(1)} %get-tuple-element.384), custom_call_target="InvertDiagBlocksLowerTriangular" | custom-call | tf_op jit(solution)/shard_map/while/body/eval_jaxpr/jit(_solve_triangular)/triangular_solve | solution.py:24
  125.0 29.7 %custom-call.93 = f32[3,128,128]{1,2,0:T(8,128)S(1)} custom-call(f32[3,128,128]{2,1,0:T(8,128)S(1)} %get-tuple-element.478), custom_call_target="InvertDiagBlocksLowerTriangular" | custom-call | tf_op jit(solution)/shard_map/while/body/eval_jaxpr/jit(_solve_triangular)/triangular_solve | solution.py:28
  243.9 149.4 %conditional.6 = (f32[384,384]{1,0:T(8,128)}, f32[384,1280]{1,0:T(8,128)}, f32[384,896]{1,0:T(8,128)}, f32[384,1280]{1,0:T(8,128)}, f32[384,512]{1,0:T(8,128)}) conditional(s32[]{:T(128)} %convert_element_type.67, f32[384,384]{1,0:T(8,128)S(1)} %copy.32, (f32[384,384]{0,1:T(8,128)}, f32[384,384]{0,1:T(8,128)}, f32[384,384]{0,1:T(8,128)}, ...), branch_computations={%region_6.9_spmd, %region_7.10_spmd} | conditional | flops 6447055360 | bytes 40899376 | solution.py:77
  275.7 13.2 cholesky.617
  333.2 31.3 %custom-call.66 = f32[3,128,128]{1,2,0:T(8,128)} custom-call(f32[3,128,128]{2,1,0:T(8,128)} %get-tuple-element.465), custom_call_target="InvertDiagBlocksLowerTriangular" | custom-call | tf_op jit(solution)/shard_map/cond/branch_1_fun/jit(_solve_triangular)/triangular_solve | solution.py:24
  407.2 67.8 %collective-permute-done.4 = f32[384,896]{0,1:T(8,128)} collective-permute-done((f32[384,896]{0,1:T(8,128)}, f32[384,896]{0,1:T(8,128)}, u32[]{:S(2)}, u32[]{:S(2)}) %collective-permute-start.4) | collective-permute-done | bytes 1376288 | tf_op jit(solution)/shard_map/ppermute | solution.py:12
  482.4 27.3 %collective-permute-done.6 = f32[384,384]{0,1:T(8,128)} collective-permute-done((f32[384,384]{0,1:T(8,128)}, f32[384,384]{0,1:T(8,128)}, u32[]{:S(2)}, u32[]{:S(2)}) %collective-permute-start.6) | collective-permute-done | bytes 589856 | tf_op jit(solution)/shard_map/ppermute | solution.py:12
  509.7 15.7 conditional.7
  538.5 67.5 %collective-permute-done.7 = f32[384,896]{0,1:T(8,128)} collective-permute-done((f32[384,896]{0,1:T(8,128)}, f32[384,896]{0,1:T(8,128)}, u32[]{:S(2)}, u32[]{:S(2)}) %collective-permute-start.7) | collective-permute-done | bytes 1376288 | tf_op jit(solution)/shard_map/ppermute | solution.py:12
  619.3 15.5 conditional.8
  647.1 30.8 %collective-permute-done.10 = f32[384,896]{0,1:T(8,128)} collective-permute-done((f32[384,896]{0,1:T(8,128)}, f32[384,896]{0,1:T(8,128)}, u32[]{:S(2)}, u32[]{:S(2)}) %collective-permute-start.10) | collective-permute-done | bytes 1376288 | tf_op jit(solution)/shard_map/ppermute | solution.py:12
  684.7 16.2 collective-permute-done.12
  700.9 15.7 conditional.9
  729.5 63.0 %collective-permute-done.13 = f32[384,896]{0,1:T(8,128)} collective-permute-done((f32[384,896]{0,1:T(8,128)}, f32[384,896]{0,1:T(8,128)}, u32[]{:S(2)}, u32[]{:S(2)}) %collective-permute-start.13) | collective-permute-done | bytes 1376288 | tf_op jit(solution)/shard_map/ppermute | solution.py:12
  798.7 13.2 collective-permute-done.15
  891.4 30.3 %custom-call.87 = f32[3,128,128]{1,2,0:T(8,128)} custom-call(f32[3,128,128]{2,1,0:T(8,128)S(1)} %get-tuple-element.472), custom_call_target="InvertDiagBlocksLowerTriangular" | custom-call | tf_op jit(solution)/shard_map/jit(_solve_triangular)/triangular_solve | solution.py:28
  921.7 690.9 %all-reduce.4.cloned.1.call-done = (f32[384,384]{0,1:T(8,128)}, f32[384,128]{1,0:T(8,128)}) async-done(((f32[384,384]{0,1:T(8,128)}, f32[384,128]{1,0:T(8,128)}), (f32[384,384]{0,1:T(8,128)}, f32[384,128]{1,0:T(8,128)})) %all-reduce.4.cloned.1.call-update) | async-done | bytes 786448 | tf_op jit(solution)/shard_map/psum | solution.py:225
  1638.9 13.2 cholesky.988
  1696.3 29.5 %custom-call.86 = f32[3,128,128]{1,2,0:T(8,128)S(1)} custom-call(f32[3,128,128]{2,1,0:T(8,128)S(1)} %get-tuple-element.471), custom_call_target="InvertDiagBlocksLowerTriangular" | custom-call | tf_op jit(solution)/shard_map/jit(_solve_triangular)/triangular_solve | solution.py:28
  1750.1 30.1 %custom-call.88 = f32[3,128,128]{1,2,0:T(8,128)} custom-call(f32[3,128,128]{2,1,0:T(8,128)S(1)} %get-tuple-element.473), custom_call_target="InvertDiagBlocksLowerTriangular" | custom-call | tf_op jit(solution)/shard_map/jit(_solve_triangular)/triangular_solve | solution.py:28
  1805.7 30.3 %custom-call.89 = f32[3,128,128]{1,2,0:T(8,128)S(1)} custom-call(f32[3,128,128]{2,1,0:T(8,128)} %copy-done.44), custom_call_target="InvertDiagBlocksLowerTriangular" | custom-call | tf_op jit(solution)/shard_map/jit(_solve_triangular)/triangular_solve | solution.py:28
  1861.8 30.1 %custom-call.90 = f32[3,128,128]{1,2,0:T(8,128)} custom-call(f32[3,128,128]{2,1,0:T(8,128)S(1)} %get-tuple-element.475), custom_call_target="InvertDiagBlocksLowerTriangular" | custom-call | tf_op jit(solution)/shard_map/jit(_solve_triangular)/triangular_solve | solution.py:28
  1918.0 30.3 %custom-call.91 = f32[3,128,128]{1,2,0:T(8,128)S(1)} custom-call(f32[3,128,128]{2,1,0:T(8,128)} %copy-done.45), custom_call_target="InvertDiagBlocksLowerTriangular" | custom-call | tf_op jit(solution)/shard_map/jit(_solve_triangular)/triangular_solve | solution.py:28
  1980.5 30.1 %custom-call.92 = f32[3,128,128]{1,2,0:T(8,128)} custom-call(f32[3,128,128]{2,1,0:T(8,128)S(1)} %get-tuple-element.477), custom_call_target="InvertDiagBlocksLowerTriangular" | custom-call | tf_op jit(solution)/shard_map/jit(_solve_triangular)/triangular_solve | solution.py:28
  (520 shorter events, 787.5 us)
Async XLA Ops:
  7.2 1605.4 %all-reduce.4.cloned.1.call-start = ((), (), s32[]{:S(2)}) async-start(), calls=%async_computation | async-start | bytes 1572864 | tf_op jit(solution)/shard_map/psum | solution.py:225
  195.5 36.9 %collective-permute-start.2 = (f32[384,384]{0,1:T(8,128)}, f32[384,384]{0,1:T(8,128)}, u32[]{:S(2)}, u32[]{:S(2)}) collective-permute-start(f32[384,384]{0,1:T(8,128)} %fusion.208), channel_id=1, source_target_pairs={{1,0},{2,1},{3,2},{4,3},{5,4},{6,5},{7,6},{8,7},{9,8},{10,9},{11,1... | collective-permute-start | bytes 1769480 | tf_op jit(solution)/shard_map/ppermute | solution.py:12
  203.6 30.9 %collective-permute-start = (f32[384,384]{0,1:T(8,128)}, f32[384,384]{0,1:T(8,128)}, u32[]{:S(2)}, u32[]{:S(2)}) collective-permute-start(f32[384,384]{0,1:T(8,128)} %fusion.210), channel_id=1, source_target_pairs={{1,0},{2,1},{3,2},{4,3},{5,4},{6,5},{7,6},{8,7},{9,8},{10,9},{11,1... | collective-permute-start | bytes 1769480 | tf_op jit(solution)/shard_map/ppermute | solution.py:12
  208.4 22.8 %collective-permute-start.3 = (f32[384,128]{0,1:T(8,128)}, f32[384,128]{0,1:T(8,128)}, u32[]{:S(2)}, u32[]{:S(2)}) collective-permute-start(f32[384,128]{0,1:T(8,128)} %neg.46), channel_id=1, source_target_pairs={{1,0},{2,1},{3,2},{4,3},{5,4},{6,5},{7,6},{8,7},{9,8},{10,9},{11,1... | collective-permute-start | bytes 589832 | tf_op jit(solution)/shard_map/ppermute | solution.py:12
  212.8 31.1 %collective-permute-start.1 = (f32[384,384]{0,1:T(8,128)}, f32[384,384]{0,1:T(8,128)}, u32[]{:S(2)}, u32[]{:S(2)}) collective-permute-start(f32[384,384]{0,1:T(8,128)} %neg.42), channel_id=1, source_target_pairs={{1,0},{2,1},{3,2},{4,3},{5,4},{6,5},{7,6},{8,7},{9,8},{10,9},{11,1... | collective-permute-start | bytes 1769480 | tf_op jit(solution)/shard_map/ppermute | solution.py:12
  396.1 79.0 %collective-permute-start.5 = (f32[384,1280]{0,1:T(8,128)}, f32[384,1280]{0,1:T(8,128)}, u32[]{:S(2)}, u32[]{:S(2)}) collective-permute-start(f32[384,1280]{0,1:T(8,128)} %copy.35), channel_id=1, source_target_pairs={{0,1},{1,2},{2,3},{3,4},{4,5},{5,6},{6,7},{7,8},{8,9},{9,10},{10,1... | collective-permute-start | bytes 5898248 | tf_op jit(solution)/shard_map/ppermute | solution.py:12
  400.9 74.2 %collective-permute-start.4 = (f32[384,896]{0,1:T(8,128)}, f32[384,896]{0,1:T(8,128)}, u32[]{:S(2)}, u32[]{:S(2)}) collective-permute-start(f32[384,896]{0,1:T(8,128)} %copy.34), channel_id=1, source_target_pairs={{1,0},{2,1},{3,2},{4,3},{5,4},{6,5},{7,6},{8,7},{9,8},{10,9},{11,1... | collective-permute-start | bytes 4128776 | tf_op jit(solution)/shard_map/ppermute | solution.py:12
  478.7 30.9 %collective-permute-start.6 = (f32[384,384]{0,1:T(8,128)}, f32[384,384]{0,1:T(8,128)}, u32[]{:S(2)}, u32[]{:S(2)}) collective-permute-start(f32[384,384]{0,1:T(8,128)} %get-tuple-element.767), channel_id=1, source_target_pairs={{2,0},{3,1},{4,2},{5,3},{6,4},{7,5},{8,6},{9,7},{10,8},{11,9},{12,... | collective-permute-start | bytes 1769480 | tf_op jit(solution)/shard_map/ppermute | solution.py:12
  528.3 77.8 %collective-permute-start.8 = (f32[384,1280]{0,1:T(8,128)}, f32[384,1280]{0,1:T(8,128)}, u32[]{:S(2)}, u32[]{:S(2)}) collective-permute-start(f32[384,1280]{0,1:T(8,128)} %copy.39), channel_id=1, source_target_pairs={{0,2},{1,3},{2,4},{3,5},{4,6},{5,7},{6,8},{7,9},{8,10},{9,11},{10,... | collective-permute-start | bytes 5898248 | tf_op jit(solution)/shard_map/ppermute | solution.py:12
  533.0 73.0 %collective-permute-start.7 = (f32[384,896]{0,1:T(8,128)}, f32[384,896]{0,1:T(8,128)}, u32[]{:S(2)}, u32[]{:S(2)}) collective-permute-start(f32[384,896]{0,1:T(8,128)} %copy.38), channel_id=1, source_target_pairs={{2,0},{3,1},{4,2},{5,3},{6,4},{7,5},{8,6},{9,7},{10,8},{11,9},{12,... | collective-permute-start | bytes 4128776 | tf_op jit(solution)/shard_map/ppermute | solution.py:12
  637.7 40.3 %collective-permute-start.11 = (f32[384,1280]{0,1:T(8,128)}, f32[384,1280]{0,1:T(8,128)}, u32[]{:S(2)}, u32[]{:S(2)}) collective-permute-start(f32[384,1280]{0,1:T(8,128)} %copy.43), channel_id=1, source_target_pairs={{0,4},{4,8},{8,12},{12,16},{16,20},{20,24},{24,28},{1,5},{5,9},{9,... | collective-permute-start | bytes 5898248 | tf_op jit(solution)/shard_map/ppermute | solution.py:12
  645.2 32.8 %collective-permute-start.10 = (f32[384,896]{0,1:T(8,128)}, f32[384,896]{0,1:T(8,128)}, u32[]{:S(2)}, u32[]{:S(2)}) collective-permute-start(f32[384,896]{0,1:T(8,128)} %copy.42), channel_id=1, source_target_pairs={{4,0},{8,4},{12,8},{16,12},{20,16},{24,20},{28,24},{5,1},{9,5},{13... | collective-permute-start | bytes 4128776 | tf_op jit(solution)/shard_map/ppermute | solution.py:12
  681.6 19.3 collective-permute-start.12
  719.5 73.0 %collective-permute-start.14 = (f32[384,1280]{0,1:T(8,128)}, f32[384,1280]{0,1:T(8,128)}, u32[]{:S(2)}, u32[]{:S(2)}) collective-permute-start(f32[384,1280]{0,1:T(8,128)} %copy.47), channel_id=1, source_target_pairs={{0,8},{4,12},{8,16},{12,20},{16,24},{20,28},{1,9},{5,13},{9,17},{1... | collective-permute-start | bytes 5898248 | tf_op jit(solution)/shard_map/ppermute | solution.py:12
  724.3 68.3 %collective-permute-start.13 = (f32[384,896]{0,1:T(8,128)}, f32[384,896]{0,1:T(8,128)}, u32[]{:S(2)}, u32[]{:S(2)}) collective-permute-start(f32[384,896]{0,1:T(8,128)} %copy.46), channel_id=1, source_target_pairs={{8,0},{12,4},{16,8},{20,12},{24,16},{28,20},{9,1},{13,5},{17,9},{2... | collective-permute-start | bytes 4128776 | tf_op jit(solution)/shard_map/ppermute | solution.py:12
  796.2 15.6 collective-permute-start.15
  823.1 41.5 %collective-permute-start.17 = (f32[384,1280]{0,1:T(8,128)}, f32[384,1280]{0,1:T(8,128)}, u32[]{:S(2)}, u32[]{:S(2)}) collective-permute-start(f32[384,1280]{0,1:T(8,128)} %copy.51), channel_id=1, source_target_pairs={{0,16},{4,20},{8,24},{12,28},{1,17},{5,21},{9,25},{13,29},{2,18},{... | collective-permute-start | bytes 5898248 | tf_op jit(solution)/shard_map/ppermute | solution.py:12
  828.8 31.5 %collective-permute-start.16 = (f32[384,896]{0,1:T(8,128)}, f32[384,896]{0,1:T(8,128)}, u32[]{:S(2)}, u32[]{:S(2)}) collective-permute-start(f32[384,896]{0,1:T(8,128)} %copy.50), channel_id=1, source_target_pairs={{16,0},{20,4},{24,8},{28,12},{17,1},{21,5},{25,9},{29,13},{18,2},{... | collective-permute-start | bytes 4128776 | tf_op jit(solution)/shard_map/ppermute | solution.py:12
  1737.9 43.7 %collective-permute-start.18 = (f32[384,128]{1,0:T(8,128)S(1)}, f32[384,128]{1,0:T(8,128)S(1)}, u32[]{:S(2)}, u32[]{:S(2)}) collective-permute-start(f32[384,128]{1,0:T(8,128)S(1)} %maximum_select_fusion), channel_id=1, source_target_pairs={{0,16},{4,20},{8,24},{12,28},{1,17},{5,21},{9,25},{13,29},{2,18},{... | collective-permute-start | bytes 589832 | tf_op jit(solution)/shard_map/ppermute | solution.py:12
  1794.5 46.1 %collective-permute-start.20 = (f32[384,128]{1,0:T(8,128)S(1)}, f32[384,128]{1,0:T(8,128)}, u32[]{:S(2)}, u32[]{:S(2)}) collective-permute-start(f32[384,128]{1,0:T(8,128)S(1)} %maximum_select_fusion.1), channel_id=1, source_target_pairs={{0,8},{4,12},{8,16},{12,20},{16,24},{20,28},{1,9},{5,13},{9,17},{1... | collective-permute-start | bytes 589832 | tf_op jit(solution)/shard_map/ppermute | solution.py:12
  1851.0 44.6 %collective-permute-start.22 = (f32[384,128]{1,0:T(8,128)S(1)}, f32[384,128]{1,0:T(8,128)S(1)}, u32[]{:S(2)}, u32[]{:S(2)}) collective-permute-start(f32[384,128]{1,0:T(8,128)S(1)} %maximum_select_fusion.2), channel_id=1, source_target_pairs={{0,4},{4,8},{8,12},{12,16},{16,20},{20,24},{24,28},{1,5},{5,9},{9,... | collective-permute-start | bytes 589832 | tf_op jit(solution)/shard_map/ppermute | solution.py:12
  1905.4 47.0 %collective-permute-start.24 = (f32[384,128]{1,0:T(8,128)S(1)}, f32[384,128]{1,0:T(8,128)}, u32[]{:S(2)}, u32[]{:S(2)}) collective-permute-start(f32[384,128]{1,0:T(8,128)S(1)} %maximum_select_fusion.3), channel_id=1, source_target_pairs={{0,2},{1,3},{2,4},{3,5},{4,6},{5,7},{6,8},{7,9},{8,10},{9,11},{10,... | collective-permute-start | bytes 589832 | tf_op jit(solution)/shard_map/ppermute | solution.py:12
  1948.4 14.8 collective-permute-start.25
  1969.7 47.4 %collective-permute-start.26 = (f32[384,128]{1,0:T(8,128)S(1)}, f32[384,128]{1,0:T(8,128)S(1)}, u32[]{:S(2)}, u32[]{:S(2)}) collective-permute-start(f32[384,128]{1,0:T(8,128)S(1)} %maximum_select_fusion.4), channel_id=1, source_target_pairs={{0,1},{1,2},{2,3},{3,4},{4,5},{5,6},{6,7},{7,8},{8,9},{9,10},{10,1... | collective-permute-start | bytes 589832 | tf_op jit(solution)/shard_map/ppermute | solution.py:12
  (48 other events, 1600.7 us)
Sparse Core Ops, SparseCore 0:
  882.6 729.9 all-reduce.3
where the time goes:
time: 2060 us; the launch traced here: 2050 us
  waiting for transfers between devices  1040 us (50%)
  other arithmetic  542 us (26%)
  local copies, waits for them, and re-layouts  197 us (10%)
  matrix products  129 us (6%)
  starting transfers between devices  86 us (4%)
  loops' own time  39.9 us (2%)
    psum x1, waiting for transfers between devices, body(): lax.psum((tip_terms, tip_rhs_terms), ('long', 'short'))  691 us
    ppermute x29, waiting for transfers between devices, shifted(): return lax.ppermute(block, axis, route)  345 us
    another operation x17, other arithmetic, solve_upper(): jax.scipy.linalg.solve_triangular(factor, values, lower=True, trans=1)  253 us
    ppermute x29, starting transfers between devices, shifted(): return lax.ppermute(block, axis, route)  86 us
    another operation x78, local copies, waits for them, and re-layouts, solve_upper(): jax.scipy.linalg.solve_triangular(factor, values, lower=True, trans=1)  69.3 us
    another operation x9, other arithmetic, solve_lower(): return jax.scipy.linalg.solve_triangular(factor, values, lower=True)  64.7 us
    another operation x10, other arithmetic, eliminate(): factor = jnp.linalg.cholesky(diag_item)  62.8 us
    another operation x11, other arithmetic, body(): tip_factor = jnp.linalg.cholesky(tip_total + jnp.diag(prior))  61 us
  transfers between devices with their start and end apart: 30, of which 19 were waited for; matrix products, arithmetic and copies ran while one was open for 15% of the time, Pallas kernels for 0%

commit v1 on v0

--- a/solution.py
+++ b/solution.py
@@ -222,7 +222,13 @@
     )
     tip_terms = tip_terms - final_tip[:, :tip_width]
     tip_rhs_terms = tip_rhs_terms - final_tip[:, tip_width:]
-    tip_total, tip_rhs_total = lax.psum((tip_terms, tip_rhs_terms), ("long", "short"))
+
+    def name_the_screen(frame_in, chip_axis, mesh_ax):
+        for jj in (chip_axis, mesh_ax):
+            frame_in = lax.psum(frame_in, jj)
+        return frame_in
+
+    tip_total, tip_rhs_total = name_the_screen((tip_terms, tip_rhs_terms), "short", "long")
     tip_factor = jnp.linalg.cholesky(tip_total + jnp.diag(prior))
     tip_solution = solve_upper(tip_factor, solve_lower(tip_factor, tip_rhs_total + tip_right))
     final_x = solve_upper(

time: 2060 us -> 1990 us (0.966)
  waiting for transfers between devices: 1040 us -> 977 us
    psum x1 -> x2, waiting for transfers between devices: 691 us -> 625 us  [name_the_screen(): frame_in = lax.psum(frame_in, jj)]
  transfers between devices with their start and end apart: 30 -> 31, of which waited for: 19 -> 20; matrix products, arithmetic and copies ran while one was open for 15% -> 15% of each run, Pallas kernels for 0% -> 0%
where the time goes in v1:
time: 1990 us
  waiting for transfers between devices  977 us (49%)
  other arithmetic  535 us (27%)
  local copies, waits for them, and re-layouts  192 us (10%)
  matrix products  128 us (6%)
  starting transfers between devices  85.7 us (4%)
  loops' own time  47.6 us (2%)
  between operations  20 us (1%)
    psum x2, waiting for transfers between devices, name_the_screen(): frame_in = lax.psum(frame_in, jj)  625 us
    ppermute x29, waiting for transfers between devices, shifted(): return lax.ppermute(block, axis, route)  352 us
    another operation x17, other arithmetic, solve_upper(): jax.scipy.linalg.solve_triangular(factor, values, lower=True, trans=1)  251 us
    ppermute x29, starting transfers between devices, shifted(): return lax.ppermute(block, axis, route)  85.6 us
    another operation x78, local copies, waits for them, and re-layouts, solve_upper(): jax.scipy.linalg.solve_triangular(factor, values, lower=True, trans=1)  66 us
    another operation x9, other arithmetic, solve_lower(): return jax.scipy.linalg.solve_triangular(factor, values, lower=True)  64.8 us
    another operation x11, other arithmetic, body(): tip_factor = jnp.linalg.cholesky(tip_total + jnp.diag(prior))  60.7 us
    another operation x10, other arithmetic, eliminate(): factor = jnp.linalg.cholesky(diag_item)  58.2 us
  transfers between devices with their start and end apart: 31, of which 20 were waited for; matrix products, arithmetic and copies ran while one was open for 15% of the time, Pallas kernels for 0%

profile of v1, /device:TPU:2, one launch (start us, length us, event | category | flops | bytes accessed | tf_op | source)
XLA Modules:
  0.0 1985.3 jit_solution(15055873085774078993)
XLA Ops:
  13.8 29.8 %custom-call.36 = f32[3,128,128]{1,2,0:T(8,128)S(1)} custom-call(f32[3,128,128]{2,1,0:T(8,128)S(1)} %get-tuple-element.384), custom_call_target="InvertDiagBlocksLowerTriangular" | custom-call | tf_op jit(solution)/shard_map/while/body/eval_jaxpr/jit(_solve_triangular)/triangular_solve | solution.py:24
  128.1 30.3 %custom-call.93 = f32[3,128,128]{1,2,0:T(8,128)} custom-call(f32[3,128,128]{2,1,0:T(8,128)S(1)} %get-tuple-element.478), custom_call_target="InvertDiagBlocksLowerTriangular" | custom-call | tf_op jit(solution)/shard_map/while/body/eval_jaxpr/jit(_solve_triangular)/triangular_solve | solution.py:28
  246.7 144.4 %conditional.6 = (f32[384,384]{1,0:T(8,128)}, f32[384,1280]{1,0:T(8,128)}, f32[384,896]{1,0:T(8,128)}, f32[384,1280]{1,0:T(8,128)}, f32[384,512]{1,0:T(8,128)}) conditional(s32[]{:T(128)} %convert_element_type.67, f32[384,384]{1,0:T(8,128)S(1)} %copy.32, (f32[384,384]{0,1:T(8,128)}, f32[384,384]{0,1:T(8,128)}, f32[384,384]{0,1:T(8,128)}, ...), branch_computations={%region_6.9_spmd, %region_7.10_spmd} | conditional | flops 6447055360 | bytes 41423692 | solution.py:77
  331.0 31.3 %custom-call.66 = f32[3,128,128]{1,2,0:T(8,128)} custom-call(f32[3,128,128]{2,1,0:T(8,128)} %get-tuple-element.465), custom_call_target="InvertDiagBlocksLowerTriangular" | custom-call | tf_op jit(solution)/shard_map/cond/branch_1_fun/jit(_solve_triangular)/triangular_solve | solution.py:24
  405.2 67.8 %collective-permute-done.4 = f32[384,896]{0,1:T(8,128)} collective-permute-done((f32[384,896]{0,1:T(8,128)}, f32[384,896]{0,1:T(8,128)}, u32[]{:S(2)}, u32[]{:S(2)}) %collective-permute-start.4) | collective-permute-done | bytes 1376288 | tf_op jit(solution)/shard_map/ppermute | solution.py:12
  480.3 27.3 %collective-permute-done.6 = f32[384,384]{0,1:T(8,128)} collective-permute-done((f32[384,384]{0,1:T(8,128)}, f32[384,384]{0,1:T(8,128)}, u32[]{:S(2)}, u32[]{:S(2)}) %collective-permute-start.6) | collective-permute-done | bytes 589856 | tf_op jit(solution)/shard_map/ppermute | solution.py:12
  507.5 15.8 conditional.7
  536.5 67.5 %collective-permute-done.7 = f32[384,896]{0,1:T(8,128)} collective-permute-done((f32[384,896]{0,1:T(8,128)}, f32[384,896]{0,1:T(8,128)}, u32[]{:S(2)}, u32[]{:S(2)}) %collective-permute-start.7) | collective-permute-done | bytes 1376288 | tf_op jit(solution)/shard_map/ppermute | solution.py:12
  617.2 15.5 conditional.8
  645.1 30.8 %collective-permute-done.10 = f32[384,896]{0,1:T(8,128)} collective-permute-done((f32[384,896]{0,1:T(8,128)}, f32[384,896]{0,1:T(8,128)}, u32[]{:S(2)}, u32[]{:S(2)}) %collective-permute-start.10) | collective-permute-done | bytes 1376288 | tf_op jit(solution)/shard_map/ppermute | solution.py:12
  682.7 16.2 collective-permute-done.12
  698.8 15.7 conditional.9
  727.5 63.0 %collective-permute-done.13 = f32[384,896]{0,1:T(8,128)} collective-permute-done((f32[384,896]{0,1:T(8,128)}, f32[384,896]{0,1:T(8,128)}, u32[]{:S(2)}, u32[]{:S(2)}) %collective-permute-start.13) | collective-permute-done | bytes 1376288 | tf_op jit(solution)/shard_map/ppermute | solution.py:12
  796.6 13.2 collective-permute-done.15
  809.7 16.1 conditional.10
  893.8 606.4 %all-reduce.8.cloned.1.call-done = (f32[384,384]{0,1:T(8,128)}, f32[384,128]{1,0:T(8,128)}) async-done(((f32[384,384]{0,1:T(8,128)}, f32[384,128]{1,0:T(8,128)}), (f32[384,384]{0,1:T(8,128)}, f32[384,128]{1,0:T(8,128)})) %all-reduce.8.cloned.1.call-update) | async-done | bytes 786448 | tf_op jit(solution)/shard_map/psum | solution.py:228
  1509.0 30.5 %custom-call.87 = f32[3,128,128]{1,2,0:T(8,128)} custom-call(f32[3,128,128]{2,1,0:T(8,128)S(1)} %get-tuple-element.472), custom_call_target="InvertDiagBlocksLowerTriangular" | custom-call | tf_op jit(solution)/shard_map/jit(_solve_triangular)/triangular_solve | solution.py:28
  1539.5 18.6 all-reduce.6.cloned.1.call-done
  1639.2 30.3 %custom-call.86 = f32[3,128,128]{1,2,0:T(8,128)S(1)} custom-call(f32[3,128,128]{2,1,0:T(8,128)} %copy-done.46), custom_call_target="InvertDiagBlocksLowerTriangular" | custom-call | tf_op jit(solution)/shard_map/jit(_solve_triangular)/triangular_solve | solution.py:28
  1690.0 29.5 %custom-call.88 = f32[3,128,128]{1,2,0:T(8,128)S(1)} custom-call(f32[3,128,128]{2,1,0:T(8,128)S(1)} %get-tuple-element.473), custom_call_target="InvertDiagBlocksLowerTriangular" | custom-call | tf_op jit(solution)/shard_map/jit(_solve_triangular)/triangular_solve | solution.py:28
  1744.8 29.5 %custom-call.89 = f32[3,128,128]{1,2,0:T(8,128)S(1)} custom-call(f32[3,128,128]{2,1,0:T(8,128)S(1)} %get-tuple-element.474), custom_call_target="InvertDiagBlocksLowerTriangular" | custom-call | tf_op jit(solution)/shard_map/jit(_solve_triangular)/triangular_solve | solution.py:28
  1800.3 29.5 %custom-call.90 = f32[3,128,128]{1,2,0:T(8,128)S(1)} custom-call(f32[3,128,128]{2,1,0:T(8,128)S(1)} %get-tuple-element.475), custom_call_target="InvertDiagBlocksLowerTriangular" | custom-call | tf_op jit(solution)/shard_map/jit(_solve_triangular)/triangular_solve | solution.py:28
  1856.1 29.5 %custom-call.91 = f32[3,128,128]{1,2,0:T(8,128)S(1)} custom-call(f32[3,128,128]{2,1,0:T(8,128)S(1)} %get-tuple-element.476), custom_call_target="InvertDiagBlocksLowerTriangular" | custom-call | tf_op jit(solution)/shard_map/jit(_solve_triangular)/triangular_solve | solution.py:28
  1917.3 29.5 %custom-call.92 = f32[3,128,128]{1,2,0:T(8,128)S(1)} custom-call(f32[3,128,128]{2,1,0:T(8,128)S(1)} %get-tuple-element.477), custom_call_target="InvertDiagBlocksLowerTriangular" | custom-call | tf_op jit(solution)/shard_map/jit(_solve_triangular)/triangular_solve | solution.py:28
  (515 shorter events, 797.5 us)
Async XLA Ops:
  7.2 1493.1 %all-reduce.8.cloned.1.call-start = ((), (), s32[]{:S(2)}) async-start(), calls=%async_computation.1 | async-start | bytes 1572864 | tf_op jit(solution)/shard_map/psum | solution.py:228
  198.3 36.9 %collective-permute-start.2 = (f32[384,384]{0,1:T(8,128)}, f32[384,384]{0,1:T(8,128)}, u32[]{:S(2)}, u32[]{:S(2)}) collective-permute-start(f32[384,384]{0,1:T(8,128)} %fusion.208), channel_id=1, source_target_pairs={{1,0},{2,1},{3,2},{4,3},{5,4},{6,5},{7,6},{8,7},{9,8},{10,9},{11,1... | collective-permute-start | bytes 1769480 | tf_op jit(solution)/shard_map/ppermute | solution.py:12
  206.5 30.9 %collective-permute-start = (f32[384,384]{0,1:T(8,128)}, f32[384,384]{0,1:T(8,128)}, u32[]{:S(2)}, u32[]{:S(2)}) collective-permute-start(f32[384,384]{0,1:T(8,128)} %fusion.210), channel_id=1, source_target_pairs={{1,0},{2,1},{3,2},{4,3},{5,4},{6,5},{7,6},{8,7},{9,8},{10,9},{11,1... | collective-permute-start | bytes 1769480 | tf_op jit(solution)/shard_map/ppermute | solution.py:12
  211.3 22.8 %collective-permute-start.3 = (f32[384,128]{0,1:T(8,128)}, f32[384,128]{0,1:T(8,128)}, u32[]{:S(2)}, u32[]{:S(2)}) collective-permute-start(f32[384,128]{0,1:T(8,128)} %neg.46), channel_id=1, source_target_pairs={{1,0},{2,1},{3,2},{4,3},{5,4},{6,5},{7,6},{8,7},{9,8},{10,9},{11,1... | collective-permute-start | bytes 589832 | tf_op jit(solution)/shard_map/ppermute | solution.py:12
  215.7 31.0 %collective-permute-start.1 = (f32[384,384]{0,1:T(8,128)}, f32[384,384]{0,1:T(8,128)}, u32[]{:S(2)}, u32[]{:S(2)}) collective-permute-start(f32[384,384]{0,1:T(8,128)} %neg.42), channel_id=1, source_target_pairs={{1,0},{2,1},{3,2},{4,3},{5,4},{6,5},{7,6},{8,7},{9,8},{10,9},{11,1... | collective-permute-start | bytes 1769480 | tf_op jit(solution)/shard_map/ppermute | solution.py:12
  394.0 79.0 %collective-permute-start.5 = (f32[384,1280]{0,1:T(8,128)}, f32[384,1280]{0,1:T(8,128)}, u32[]{:S(2)}, u32[]{:S(2)}) collective-permute-start(f32[384,1280]{0,1:T(8,128)} %copy.35), channel_id=1, source_target_pairs={{0,1},{1,2},{2,3},{3,4},{4,5},{5,6},{6,7},{7,8},{8,9},{9,10},{10,1... | collective-permute-start | bytes 5898248 | tf_op jit(solution)/shard_map/ppermute | solution.py:12
  398.8 74.2 %collective-permute-start.4 = (f32[384,896]{0,1:T(8,128)}, f32[384,896]{0,1:T(8,128)}, u32[]{:S(2)}, u32[]{:S(2)}) collective-permute-start(f32[384,896]{0,1:T(8,128)} %copy.34), channel_id=1, source_target_pairs={{1,0},{2,1},{3,2},{4,3},{5,4},{6,5},{7,6},{8,7},{9,8},{10,9},{11,1... | collective-permute-start | bytes 4128776 | tf_op jit(solution)/shard_map/ppermute | solution.py:12
  476.6 30.9 %collective-permute-start.6 = (f32[384,384]{0,1:T(8,128)}, f32[384,384]{0,1:T(8,128)}, u32[]{:S(2)}, u32[]{:S(2)}) collective-permute-start(f32[384,384]{0,1:T(8,128)} %get-tuple-element.769), channel_id=1, source_target_pairs={{2,0},{3,1},{4,2},{5,3},{6,4},{7,5},{8,6},{9,7},{10,8},{11,9},{12,... | collective-permute-start | bytes 1769480 | tf_op jit(solution)/shard_map/ppermute | solution.py:12
  526.2 77.8 %collective-permute-start.8 = (f32[384,1280]{0,1:T(8,128)}, f32[384,1280]{0,1:T(8,128)}, u32[]{:S(2)}, u32[]{:S(2)}) collective-permute-start(f32[384,1280]{0,1:T(8,128)} %copy.39), channel_id=1, source_target_pairs={{0,2},{1,3},{2,4},{3,5},{4,6},{5,7},{6,8},{7,9},{8,10},{9,11},{10,... | collective-permute-start | bytes 5898248 | tf_op jit(solution)/shard_map/ppermute | solution.py:12
  531.0 73.0 %collective-permute-start.7 = (f32[384,896]{0,1:T(8,128)}, f32[384,896]{0,1:T(8,128)}, u32[]{:S(2)}, u32[]{:S(2)}) collective-permute-start(f32[384,896]{0,1:T(8,128)} %copy.38), channel_id=1, source_target_pairs={{2,0},{3,1},{4,2},{5,3},{6,4},{7,5},{8,6},{9,7},{10,8},{11,9},{12,... | collective-permute-start | bytes 4128776 | tf_op jit(solution)/shard_map/ppermute | solution.py:12
  635.6 40.3 %collective-permute-start.11 = (f32[384,1280]{0,1:T(8,128)}, f32[384,1280]{0,1:T(8,128)}, u32[]{:S(2)}, u32[]{:S(2)}) collective-permute-start(f32[384,1280]{0,1:T(8,128)} %copy.43), channel_id=1, source_target_pairs={{0,4},{4,8},{8,12},{12,16},{16,20},{20,24},{24,28},{1,5},{5,9},{9,... | collective-permute-start | bytes 5898248 | tf_op jit(solution)/shard_map/ppermute | solution.py:12
  643.2 32.8 %collective-permute-start.10 = (f32[384,896]{0,1:T(8,128)}, f32[384,896]{0,1:T(8,128)}, u32[]{:S(2)}, u32[]{:S(2)}) collective-permute-start(f32[384,896]{0,1:T(8,128)} %copy.42), channel_id=1, source_target_pairs={{4,0},{8,4},{12,8},{16,12},{20,16},{24,20},{28,24},{5,1},{9,5},{13... | collective-permute-start | bytes 4128776 | tf_op jit(solution)/shard_map/ppermute | solution.py:12
  679.6 19.3 collective-permute-start.12
  717.5 73.0 %collective-permute-start.14 = (f32[384,1280]{0,1:T(8,128)}, f32[384,1280]{0,1:T(8,128)}, u32[]{:S(2)}, u32[]{:S(2)}) collective-permute-start(f32[384,1280]{0,1:T(8,128)} %copy.47), channel_id=1, source_target_pairs={{0,8},{4,12},{8,16},{12,20},{16,24},{20,28},{1,9},{5,13},{9,17},{1... | collective-permute-start | bytes 5898248 | tf_op jit(solution)/shard_map/ppermute | solution.py:12
  722.2 68.2 %collective-permute-start.13 = (f32[384,896]{0,1:T(8,128)}, f32[384,896]{0,1:T(8,128)}, u32[]{:S(2)}, u32[]{:S(2)}) collective-permute-start(f32[384,896]{0,1:T(8,128)} %copy.46), channel_id=1, source_target_pairs={{8,0},{12,4},{16,8},{20,12},{24,16},{28,20},{9,1},{13,5},{17,9},{2... | collective-permute-start | bytes 4128776 | tf_op jit(solution)/shard_map/ppermute | solution.py:12
  794.1 15.6 collective-permute-start.15
  828.7 41.5 %collective-permute-start.17 = (f32[384,1280]{0,1:T(8,128)}, f32[384,1280]{0,1:T(8,128)}, u32[]{:S(2)}, u32[]{:S(2)}) collective-permute-start(f32[384,1280]{0,1:T(8,128)} %copy.51), channel_id=1, source_target_pairs={{0,16},{4,20},{8,24},{12,28},{1,17},{5,21},{9,25},{13,29},{2,18},{... | collective-permute-start | bytes 5898248 | tf_op jit(solution)/shard_map/ppermute | solution.py:12
  834.4 31.5 %collective-permute-start.16 = (f32[384,896]{0,1:T(8,128)}, f32[384,896]{0,1:T(8,128)}, u32[]{:S(2)}, u32[]{:S(2)}) collective-permute-start(f32[384,896]{0,1:T(8,128)} %copy.50), channel_id=1, source_target_pairs={{16,0},{20,4},{24,8},{28,12},{17,1},{21,5},{25,9},{29,13},{18,2},{... | collective-permute-start | bytes 4128776 | tf_op jit(solution)/shard_map/ppermute | solution.py:12
  887.1 671.0 %all-reduce.6.cloned.1.call-start = ((), (), s32[]{:S(2)}) async-start(), calls=%async_computation | async-start | bytes 1572864 | tf_op jit(solution)/shard_map/psum | solution.py:228
  1678.2 42.7 %collective-permute-start.18 = (f32[384,128]{1,0:T(8,128)S(1)}, f32[384,128]{1,0:T(8,128)}, u32[]{:S(2)}, u32[]{:S(2)}) collective-permute-start(f32[384,128]{1,0:T(8,128)S(1)} %maximum_select_fusion), channel_id=1, source_target_pairs={{0,16},{4,20},{8,24},{12,28},{1,17},{5,21},{9,25},{13,29},{2,18},{... | collective-permute-start | bytes 589832 | tf_op jit(solution)/shard_map/ppermute | solution.py:12
  1733.8 44.7 %collective-permute-start.20 = (f32[384,128]{1,0:T(8,128)S(1)}, f32[384,128]{1,0:T(8,128)}, u32[]{:S(2)}, u32[]{:S(2)}) collective-permute-start(f32[384,128]{1,0:T(8,128)S(1)} %maximum_select_fusion.1), channel_id=1, source_target_pairs={{0,8},{4,12},{8,16},{12,20},{16,24},{20,28},{1,9},{5,13},{9,17},{1... | collective-permute-start | bytes 589832 | tf_op jit(solution)/shard_map/ppermute | solution.py:12
  1789.3 44.1 %collective-permute-start.22 = (f32[384,128]{1,0:T(8,128)S(1)}, f32[384,128]{1,0:T(8,128)}, u32[]{:S(2)}, u32[]{:S(2)}) collective-permute-start(f32[384,128]{1,0:T(8,128)S(1)} %maximum_select_fusion.2), channel_id=1, source_target_pairs={{0,4},{4,8},{8,12},{12,16},{16,20},{20,24},{24,28},{1,5},{5,9},{9,... | collective-permute-start | bytes 589832 | tf_op jit(solution)/shard_map/ppermute | solution.py:12
  1843.1 45.7 %collective-permute-start.24 = (f32[384,128]{1,0:T(8,128)S(1)}, f32[384,128]{1,0:T(8,128)}, u32[]{:S(2)}, u32[]{:S(2)}) collective-permute-start(f32[384,128]{1,0:T(8,128)S(1)} %maximum_select_fusion.3), channel_id=1, source_target_pairs={{0,2},{1,3},{2,4},{3,5},{4,6},{5,7},{6,8},{7,9},{8,10},{9,11},{10,... | collective-permute-start | bytes 589832 | tf_op jit(solution)/shard_map/ppermute | solution.py:12
  1906.6 46.6 %collective-permute-start.26 = (f32[384,128]{1,0:T(8,128)S(1)}, f32[384,128]{1,0:T(8,128)}, u32[]{:S(2)}, u32[]{:S(2)}) collective-permute-start(f32[384,128]{1,0:T(8,128)S(1)} %maximum_select_fusion.4), channel_id=1, source_target_pairs={{0,1},{1,2},{2,3},{3,4},{4,5},{5,6},{6,7},{7,8},{8,9},{9,10},{10,1... | collective-permute-start | bytes 589832 | tf_op jit(solution)/shard_map/ppermute | solution.py:12
  (45 other events, 1460.6 us)
Sparse Core Ops, SparseCore 0:
  887.3 612.9 all-reduce.7
  1503.5 54.6 all-reduce.5
